TPU v7x, 32 devices: a whole 2x2x4 slice. The times are simulated.
32 devices in a mesh: row: 4 (over y, x), col: 8 (over z, core).
Axes of the slice: x: 2, y: 2, z: 4, core: 2. Of those that a mesh axis runs over, the one named last changes fastest.
Arguments:
- tokens: bfloat16 [8192, 4096], P(('row', 'col')), may hold values from -6 to 6
- grad_out: bfloat16 [8192, 512], P(('row', 'col')), may hold values from -0.375 to 0.375
- residual: bfloat16 [32, 2048, 1024], P(('row', 'col')), may hold values from -6 to 6
- momentum: float32 [2048, 1024], P(('row', 'col')), may hold values from -4 to 4
- kept_blocks: int32 [4, 8, 5, 128], P('row', 'col'), may hold values from 0 to 2047, as said below
- kept_counts: int32 [4, 8, 5], P('row', 'col'), may hold values from 1 to 128, as said below
Outputs:
- residual_out: bfloat16 [32, 2048, 1024], P(('row', 'col'))
- momentum_out: float32 [2048, 1024], P(('row', 'col'))
Inputs may be any that keep to these rules, and one draw needn't show every extreme that they name: `kept_blocks`: valid entries of one list are distinct. Lists of section t are equal on all replicas that share row and col // 2 ** (t + 1) for t < 3, and on all replicas that share row // 2 ** (u + 1) for section 3 + u. Padding entries are arbitrary block numbers. `kept_counts`: equal within each section's group as for the lists; the largest is reached in every draw.
All inputs are finite; a program needn't handle non-finite values.
Results may differ from a plain program's by a relative error of at most 0.001.
Values sent between devices are 32-bit elements; how exact they have to be, the bound alone decides.
A program may use at most 128 MiB of HBM per device.

v0:
```python
import jax
import jax.numpy as jnp
from jax import lax
from jax.sharding import PartitionSpec as P

decay_rate = 0.9


def partner(value, axis, apart):
    mask = 2**apart
    pairs = [(source, source ^ mask) for source in range(lax.axis_size(axis))]
    return lax.ppermute(value, axis, pairs)


def relist(summed, marked_from, marked_into):
    match_table = (marked_into[:, None] == marked_from[None, :]).astype(jnp.float32)
    return jnp.dot(
        match_table, summed, preferred_element_type=jnp.float32, precision=lax.Precision.HIGHEST
    )


def body(tokens, grad_out, residual, momentum, kept_blocks, kept_counts):
    row_count = lax.axis_size("row")
    col_count = lax.axis_size("col")
    col_sections = col_count.bit_length() - 1
    row_sections = row_count.bit_length() - 1
    block_count = residual.shape[1]
    block_width = residual.shape[2]
    weight_grad = lax.dot_general(
        tokens, grad_out, (((0,), (0,)), ((), ())), preferred_element_type=jnp.float32
    )
    accumulated = weight_grad.reshape(block_count, block_width) + residual[0].astype(jnp.float32)
    block_lists = kept_blocks[0, 0]
    block_counts = kept_counts[0, 0]
    capacity = block_lists.shape[1]
    slot_ids = jnp.arange(capacity, dtype=jnp.int32)
    is_valid = slot_ids[None, :] < block_counts[:, None]
    marked_high = jnp.where(is_valid, block_lists, block_count)
    marked_low = jnp.where(is_valid, block_lists, -1)
    block_ids = jnp.arange(block_count, dtype=jnp.int32)
    member = jnp.any(marked_high[:, :, None] == block_ids[None, None, :], axis=1)
    kept_mask = jnp.all(member, axis=0)
    residual_out = jnp.where(kept_mask[:, None], 0.0, accumulated).astype(jnp.bfloat16)[None]
    shard_rows = momentum.shape[0]
    owner_id = lax.axis_index("row") * col_count + lax.axis_index("col")
    own_ids = owner_id * shard_rows + jnp.arange(shard_rows, dtype=jnp.int32)
    section_total = col_sections + row_sections
    packed = accumulated[block_lists[0]] * is_valid[0][:, None].astype(jnp.float32)
    summed = packed
    section_id = 0
    for bit_index in range(col_sections):
        partner_part = partner(packed, "col", bit_index)
        summed = packed + partner_part
        packed = relist(summed, marked_high[section_id], marked_low[section_id + 1])
        section_id = section_id + 1
    for bit_index in range(row_sections):
        partner_part = partner(packed, "row", bit_index)
        summed = packed + partner_part
        if section_id + 1 < section_total:
            packed = relist(summed, marked_high[section_id], marked_low[section_id + 1])
        section_id = section_id + 1
    total_shard = relist(summed, marked_high[section_total - 1], own_ids)
    momentum_out = decay_rate * momentum + total_shard / (row_count * col_count)
    return (residual_out, momentum_out)


def solution(mesh):
    in_specs = (
        P(("row", "col"), None),
        P(("row", "col"), None),
        P(("row", "col"), None, None),
        P(("row", "col"), None),
        P("row", "col", None, None),
        P("row", "col", None),
    )
    out_specs = (P(("row", "col"), None, None), P(("row", "col"), None))
    return jax.shard_map(body, mesh=mesh, in_specs=in_specs, out_specs=out_specs, check_vma=False)
```

profile of v0, /device:TPU:0, one launch (start us, length us, event | category | flops | bytes accessed | tf_op | source)
XLA Modules:
  0.0 103.2 jit_solution(7297191924113394719)
XLA Ops:
  0.6 0.0 copy-start
  0.6 1.6 %copy-done = bf16[256,4096]{1,0:T(8,128)(2,1)S(1)} copy-done((bf16[256,4096]{1,0:T(8,128)(2,1)S(1)}, bf16[256,4096]{1,0:T(8,128)(2,1)}, u32[]{:S(2)}) %copy-start) | copy-done | bytes 2097176
  2.2 5.5 %fusion.31 = f32[4096,512]{1,0:T(8,128)} fusion(bf16[256,4096]{1,0:T(8,128)(2,1)S(1)} %copy-done, bf16[256,512]{1,0:T(8,128)(2,1)} %param.7), kind=kOutput, calls=%fused_computation.53 | convolution fusion | flops 1073741824 | bytes 10747904 | tf_op jit(solution)/shard_map/dot_general | solution.py:29
  7.7 0.0 copy-start.2
  7.7 0.0 copy-start.3
  7.7 9.9 %reshape.95 = f32[2048,1024]{1,0:T(8,128)} reshape(f32[4096,512]{1,0:T(8,128)} %fusion.31) | data formatting | bytes 16777216 | tf_op jit(solution)/shard_map/reshape | solution.py:32
  17.6 0.0 copy-done.2
  17.6 0.0 copy-done.3
  17.7 0.1 iota_compare_fusion.1
  17.7 10.0 %fusion.2 = f32[2048,1024]{1,0:T(8,128)} fusion(f32[2048,1024]{1,0:T(8,128)} %reshape.95, bf16[1,2048,1024]{2,1,0:T(8,128)(2,1)} %param.8), kind=kLoop, calls=%fused_computation.5 | loop fusion | flops 4194304 | bytes 20971520 | tf_op jit(solution)/shard_map/add | solution.py:32
  27.7 4.4 %gather_fusion = f32[128,1024]{1,0:T(8,128)S(1)} fusion(f32[2048,1024]{1,0:T(8,128)} %fusion.2, s32[1024]{0:T(1024)S(1)} %pad_clamp_fusion), kind=kCustom, calls=%fused_computation | custom fusion | bytes 1049088 | tf_op jit(solution)/shard_map/gather | solution.py:48
  32.2 0.1 broadcast_multiply_fusion
  32.3 0.6 collective-permute-start
  32.8 0.1 bitcast_select_fusion
  32.9 1.5 %collective-permute-done = f32[128,1024]{1,0:T(8,128)S(1)} collective-permute-done((f32[128,1024]{1,0:T(8,128)S(1)}, f32[128,1024]{1,0:T(8,128)S(1)}, u32[]{:S(2)}, u32[]{:S(2)}) %collective-permute-start) | collective-permute-done | bytes 524320 | tf_op jit(solution)/shard_map/ppermute | solution.py:12
  34.4 0.4 fusion.12
  34.8 3.0 %collective-permute-start.1 = (f32[128,1024]{1,0:T(8,128)S(1)}, f32[128,1024]{1,0:T(8,128)S(1)}, u32[]{:S(2)}, u32[]{:S(2)}) collective-permute-start(f32[128,1024]{1,0:T(8,128)S(1)} %fusion.12), channel_id=1, source_target_pairs={{0,2},{1,3},{2,0},{3,1},{4,6},{5,7},{6,4},{7,5},{8,10},{9,11},{10,... | collective-permute-start | bytes 1572872 | tf_op jit(solution)/shard_map/ppermute | solution.py:12
  37.8 12.2 %collective-permute-done.1 = f32[128,1024]{1,0:T(8,128)S(1)} collective-permute-done((f32[128,1024]{1,0:T(8,128)S(1)}, f32[128,1024]{1,0:T(8,128)S(1)}, u32[]{:S(2)}, u32[]{:S(2)}) %collective-permute-start.1) | collective-permute-done | bytes 524320 | tf_op jit(solution)/shard_map/ppermute | solution.py:12
  50.0 0.4 fusion.10
  50.4 2.8 %collective-permute-start.2 = (f32[128,1024]{1,0:T(8,128)S(1)}, f32[128,1024]{1,0:T(8,128)S(1)}, u32[]{:S(2)}, u32[]{:S(2)}) collective-permute-start(f32[128,1024]{1,0:T(8,128)S(1)} %fusion.10), channel_id=1, source_target_pairs={{0,4},{1,5},{2,6},{3,7},{4,0},{5,1},{6,2},{7,3},{8,12},{9,13},{10,... | collective-permute-start | bytes 1572872 | tf_op jit(solution)/shard_map/ppermute | solution.py:12
  53.3 22.8 %collective-permute-done.2 = f32[128,1024]{1,0:T(8,128)S(1)} collective-permute-done((f32[128,1024]{1,0:T(8,128)S(1)}, f32[128,1024]{1,0:T(8,128)S(1)}, u32[]{:S(2)}, u32[]{:S(2)}) %collective-permute-start.2) | collective-permute-done | bytes 524320 | tf_op jit(solution)/shard_map/ppermute | solution.py:12
  76.0 0.4 fusion.8
  76.5 1.4 %collective-permute-start.3 = (f32[128,1024]{1,0:T(8,128)S(1)}, f32[128,1024]{1,0:T(8,128)S(1)}, u32[]{:S(2)}, u32[]{:S(2)}) collective-permute-start(f32[128,1024]{1,0:T(8,128)S(1)} %fusion.8), channel_id=1, source_target_pairs={{0,8},{8,0},{16,24},{24,16},{1,9},{9,1},{17,25},{25,17},{2,10},{10... | collective-permute-start | bytes 1572872 | tf_op jit(solution)/shard_map/ppermute | solution.py:12
  77.9 9.9 %reshape.94 = f32[1,2048,1024]{2,1,0:T(8,128)} reshape(f32[4096,512]{1,0:T(8,128)} %fusion.31) | data formatting | bytes 16777216 | tf_op jit(solution)/shard_map/reshape | solution.py:32
  87.8 1.2 %fusion.3 = pred[5,2048]{1,0:T(8,128)(4,1)S(1)} fusion(s32[5,128]{1,0:T(8,128)S(1)} %get-tuple-element.12), kind=kLoop, calls=%fused_computation.7 | loop fusion | flops 2611200 | bytes 12800 | tf_op jit(solution)/shard_map/reduce_or | solution.py:41
  89.0 0.5 collective-permute-done.3
  89.5 0.4 fusion.6
  89.9 0.0 copy-start.1
  89.9 1.4 %collective-permute-start.4 = (f32[128,1024]{1,0:T(8,128)S(1)}, f32[128,1024]{1,0:T(8,128)S(1)}, u32[]{:S(2)}, u32[]{:S(2)}) collective-permute-start(f32[128,1024]{1,0:T(8,128)S(1)} %fusion.6), channel_id=1, source_target_pairs={{0,16},{8,24},{16,0},{24,8},{1,17},{9,25},{17,1},{25,9},{2,18},{10... | collective-permute-start | bytes 1572872 | tf_op jit(solution)/shard_map/ppermute | solution.py:12
  91.3 7.1 %fusion.1 = bf16[1,2048,1024]{2,1,0:T(8,128)(2,1)} fusion(f32[1,2048,1024]{2,1,0:T(8,128)} %reshape.94, bf16[1,2048,1024]{2,1,0:T(8,128)(2,1)} %param.8, pred[2048]{0:T(1024)(128)(4,1)S(1)} %reduce_and.9), kind=kLoop, calls=%fused_computation.4 | loop fusion | flops 8388608 | bytes 16779264 | tf_op jit(solution)/shard_map/convert_element_type | solution.py:43
  98.4 3.7 %collective-permute-done.4 = f32[128,1024]{1,0:T(8,128)S(1)} collective-permute-done((f32[128,1024]{1,0:T(8,128)S(1)}, f32[128,1024]{1,0:T(8,128)S(1)}, u32[]{:S(2)}, u32[]{:S(2)}) %collective-permute-start.4) | collective-permute-done | bytes 524320 | tf_op jit(solution)/shard_map/ppermute | solution.py:12
  102.1 0.0 copy-done.1
  102.1 1.1 %fusion.4 = f32[64,1024]{1,0:T(8,128)} fusion(f32[128,1024]{1,0:T(8,128)S(1)} %fusion.6, f32[128,1024]{1,0:T(8,128)S(1)} %collective-permute-done.4, f32[64,1024]{1,0:T(8,128)S(1)} %copy-done.1, s32[128]{0:T(128)S(1)} %get-tuple-element.17, s32[64]{0:T(128)S(1)} %iota_add_fusion), kind=kOutput, calls=%fused_computation.9 | convolution fusion | flops 100999168 | bytes 1573632 | tf_op jit(solution)/shard_map/dot_general | solution.py:17
  (6 shorter events, 0.1 us)
Async XLA Ops:
  0.6 1.6 %copy-start = (bf16[256,4096]{1,0:T(8,128)(2,1)S(1)}, bf16[256,4096]{1,0:T(8,128)(2,1)}, u32[]{:S(2)}) copy-start(bf16[256,4096]{1,0:T(8,128)(2,1)} %param.6) | copy-start | bytes 6291460
  7.7 9.9 %copy-start.2 = (s32[1,1,5,128]{3,1,2,0:T(1,128)S(1)}, s32[1,1,5,128]{3,1,2,0:T(1,128)}, u32[]{:S(2)}) copy-start(s32[1,1,5,128]{3,1,2,0:T(1,128)} %param.10) | copy-start | bytes 7684
  7.7 10.0 %copy-start.3 = (s32[1,1,5]{2,1,0:T(1,128)S(1)}, s32[1,1,5]{2,1,0:T(1,128)}, u32[]{:S(2)}) copy-start(s32[1,1,5]{2,1,0:T(1,128)} %param.11) | copy-start | bytes 64
  32.3 2.1 %collective-permute-start = (f32[128,1024]{1,0:T(8,128)S(1)}, f32[128,1024]{1,0:T(8,128)S(1)}, u32[]{:S(2)}, u32[]{:S(2)}) collective-permute-start(f32[128,1024]{1,0:T(8,128)S(1)} %broadcast_multiply_fusion), channel_id=1, source_target_pairs={{0,1},{1,0},{2,3},{3,2},{4,5},{5,4},{6,7},{7,6},{8,9},{9,8},{10,11... | collective-permute-start | bytes 1572872 | tf_op jit(solution)/shard_map/ppermute | solution.py:12
  34.8 15.2 %collective-permute-start.1 = (f32[128,1024]{1,0:T(8,128)S(1)}, f32[128,1024]{1,0:T(8,128)S(1)}, u32[]{:S(2)}, u32[]{:S(2)}) collective-permute-start(f32[128,1024]{1,0:T(8,128)S(1)} %fusion.12), channel_id=1, source_target_pairs={{0,2},{1,3},{2,0},{3,1},{4,6},{5,7},{6,4},{7,5},{8,10},{9,11},{10,... | collective-permute-start | bytes 1572872 | tf_op jit(solution)/shard_map/ppermute | solution.py:12
  50.4 25.6 %collective-permute-start.2 = (f32[128,1024]{1,0:T(8,128)S(1)}, f32[128,1024]{1,0:T(8,128)S(1)}, u32[]{:S(2)}, u32[]{:S(2)}) collective-permute-start(f32[128,1024]{1,0:T(8,128)S(1)} %fusion.10), channel_id=1, source_target_pairs={{0,4},{1,5},{2,6},{3,7},{4,0},{5,1},{6,2},{7,3},{8,12},{9,13},{10,... | collective-permute-start | bytes 1572872 | tf_op jit(solution)/shard_map/ppermute | solution.py:12
  76.5 13.0 %collective-permute-start.3 = (f32[128,1024]{1,0:T(8,128)S(1)}, f32[128,1024]{1,0:T(8,128)S(1)}, u32[]{:S(2)}, u32[]{:S(2)}) collective-permute-start(f32[128,1024]{1,0:T(8,128)S(1)} %fusion.8), channel_id=1, source_target_pairs={{0,8},{8,0},{16,24},{24,16},{1,9},{9,1},{17,25},{25,17},{2,10},{10... | collective-permute-start | bytes 1572872 | tf_op jit(solution)/shard_map/ppermute | solution.py:12
  89.9 12.2 %copy-start.1 = (f32[64,1024]{1,0:T(8,128)S(1)}, f32[64,1024]{1,0:T(8,128)}, u32[]{:S(2)}) copy-start(f32[64,1024]{1,0:T(8,128)} %param.9) | copy-start | bytes 786436
  89.9 12.2 %collective-permute-start.4 = (f32[128,1024]{1,0:T(8,128)S(1)}, f32[128,1024]{1,0:T(8,128)S(1)}, u32[]{:S(2)}, u32[]{:S(2)}) collective-permute-start(f32[128,1024]{1,0:T(8,128)S(1)} %fusion.6), channel_id=1, source_target_pairs={{0,16},{8,24},{16,0},{24,8},{1,17},{9,25},{17,1},{25,9},{2,18},{10... | collective-permute-start | bytes 1572872 | tf_op jit(solution)/shard_map/ppermute | solution.py:12
where the time goes:
time: 104 us; the launch traced here: 103 us
  waiting for transfers between devices  40.6 us (39%)
  local copies, waits for them, and re-layouts  25.9 us (25%)
  other arithmetic  18.6 us (18%)
  starting transfers between devices  9.16 us (9%)
  matrix products  8.23 us (8%)
    ppermute x5, waiting for transfers between devices, partner(): return lax.ppermute(value, axis, pairs)  40.6 us
    reshape x2, local copies, waits for them, and re-layouts, body(): weight_grad.reshape(block_count, block_width)  19.8 us
    add x1, other arithmetic, body(): weight_grad.reshape(block_count, block_width)  9.98 us
    ppermute x5, starting transfers between devices, partner(): return lax.ppermute(value, axis, pairs)  9.16 us
    convert_element_type x1, other arithmetic, body(): jnp.where(kept_mask[:, None], 0.0, accumulated).astype(jnp.bfloat16)[None]  7.15 us
    dot_general x1, matrix products, body(): lax.dot_general(tokens, grad_out, (((0,), (0,)), ((), ())), preferred_ele...  5.47 us
    gather x1, local copies, waits for them, and re-layouts, body(): accumulated[block_lists[0]] * is_valid[0][:, None].astype(jnp.float32)  4.42 us
    dot_general x5, matrix products, relist(): jnp.dot(match_table, summed, preferred_element_type=jnp.float32, precisio...  2.76 us
  transfers between devices with their start and end apart: 5, of which 5 were waited for; matrix products, arithmetic and copies ran while one was open for 18% of the time, Pallas kernels for 0%

commit v1 on v0

v1 whole, which is shorter than its diff:
```python
import functools

import jax
import jax.numpy as jnp
from jax import lax
from jax.experimental import pallas as pl
from jax.experimental.pallas import tpu as pltpu
from jax.sharding import PartitionSpec as P

decay_rate = 0.9
MESH = pl.DeviceIdType.MESH
LANES = 128


def column_of(row):
    n = row.shape[1]
    down = lax.broadcasted_iota(jnp.int32, (n, n), 0)
    along = lax.broadcasted_iota(jnp.int32, (n, n), 1)
    spread = jnp.broadcast_to(row, (n, n))
    return jnp.sum(jnp.where(down == along, spread, 0), axis=1, keepdims=True)


def local_kernel(steps, last_ref, tokens_ref, grad_ref, residual_ref, lists_ref, counts_ref,
                 out_ref, packed_ref, acc, marks, gathered):
    step = pl.program_id(0)
    chunk = residual_ref.shape[0]
    sections, capacity = lists_ref.shape
    half = grad_ref.shape[1]

    @pl.when(step == 0)
    def _():
        slot_ids = lax.broadcasted_iota(jnp.int32, (1, capacity), 1)
        last = lists_ref[sections - 1:sections, :]
        kept = jnp.where(slot_ids < counts_ref[sections - 1], 1, 0)
        for section in range(sections - 1):
            row = jnp.where(slot_ids < counts_ref[section], lists_ref[section:section + 1, :], -1)
            hits = jnp.where(column_of(row) == last, 1, 0)
            kept = kept * jnp.max(hits, axis=0, keepdims=True)
        marks[...] = jnp.where(kept > 0, last, -1)

    sub = 256
    out_ids = lax.broadcasted_iota(jnp.int32, (sub, sub), 0)
    in_ids = lax.broadcasted_iota(jnp.int32, (sub, sub), 1)
    source = jnp.where(out_ids < sub // 2, 2 * out_ids, 2 * out_ids - sub + 1)
    shuffle = (source == in_ids).astype(jnp.float32).astype(jnp.bfloat16)
    pieces = 2 * chunk // sub
    for piece in range(pieces):
        part = tokens_ref[:, piece * sub:(piece + 1) * sub]
        turned = lax.dot_general(
            shuffle, part, (((1,), (1,)), ((), ())), preferred_element_type=jnp.float32
        ).astype(jnp.bfloat16)
        grads = jnp.dot(turned, grad_ref[...], preferred_element_type=jnp.float32)
        rows = slice(piece * (sub // 2), (piece + 1) * (sub // 2))
        block_ids = step * chunk + piece * (sub // 2) + lax.broadcasted_iota(
            jnp.int32, (sub // 2, capacity), 0)
        kept = jnp.max(jnp.where(block_ids == marks[...], 1, 0), axis=1, keepdims=True) > 0
        for side in range(2):
            columns = slice(side * half, (side + 1) * half)
            total = grads[side * (sub // 2):(side + 1) * (sub // 2)] + residual_ref[rows, columns].astype(jnp.float32)
            acc[pl.ds(step * chunk + piece * (sub // 2), sub // 2), columns] = total
            out_ref[rows, columns] = jnp.where(kept, 0.0, total).astype(jnp.bfloat16)

    @pl.when(step == steps - 1)
    def _():
        def fetch(slot, carry):
            gathered[pl.ds(slot, 1), :] = acc[pl.ds(last_ref[slot], 1), :]
            return carry

        lax.fori_loop(0, capacity, fetch, 0, unroll=8)
        keep = column_of(marks[...]) >= 0
        for lane in range(packed_ref.shape[0]):
            packed_ref[lane] = jnp.where(keep, gathered[:, lane * LANES:(lane + 1) * LANES], 0.0)


def local_part(tokens, grad_out, residual, lists, counts):
    token_count, features = tokens.shape
    half = grad_out.shape[1]
    blocks, width = residual.shape
    sections, capacity = lists.shape
    chunk = 256
    steps = blocks // chunk
    return pl.pallas_call(
        functools.partial(local_kernel, steps),
        grid_spec=pltpu.PrefetchScalarGridSpec(
            num_scalar_prefetch=1,
            grid=(steps,),
            in_specs=[
                pl.BlockSpec((token_count, 2 * chunk), lambda i, s: (0, i)),
                pl.BlockSpec((token_count, half), lambda i, s: (0, 0)),
                pl.BlockSpec((chunk, width), lambda i, s: (i, 0)),
                pl.BlockSpec((sections, capacity), lambda i, s: (0, 0)),
                pl.BlockSpec(memory_space=pltpu.SMEM),
            ],
            out_specs=[
                pl.BlockSpec((chunk, width), lambda i, s: (i, 0)),
                pl.BlockSpec((width // LANES, capacity, LANES), lambda i, s: (0, 0, 0)),
            ],
            scratch_shapes=[
                pltpu.VMEM((blocks, width), jnp.float32),
                pltpu.VMEM((1, capacity), jnp.int32),
                pltpu.VMEM((capacity, width), jnp.float32),
            ],
        ),
        out_shape=[
            jax.ShapeDtypeStruct((blocks, width), jnp.bfloat16),
            jax.ShapeDtypeStruct((width // LANES, capacity, LANES), jnp.float32),
        ],
        compiler_params=pltpu.CompilerParams(dimension_semantics=("arbitrary",)),
        name="local",
    )(lists[sections - 1], tokens, grad_out, residual, lists, counts)


def sum_kernel(rows, zs, packed_ref, momentum_ref, last_ref, count_ref, out_ref,
               core_in, half, row_in, part, z_in, full,
               a_send, a_recv, b_send, b_recv, c_send, c_recv,
               d_send, d_recv, e_send, e_recv, f_send, f_recv):
    row = lax.axis_index("row")
    col = lax.axis_index("col")
    z = col // 2
    core = col % 2
    other = 1 - core
    mate = (row, z * 2 + other)

    def row_peer(i):
        return (lax.rem(row + i, rows), col)

    def z_peer(i):
        return (row, lax.rem(z + i, zs) * 2 + core)

    def send(src, dst, send_sem, recv_sem, peer):
        copy = pltpu.make_async_remote_copy(
            src_ref=src, dst_ref=dst, send_sem=send_sem, recv_sem=recv_sem,
            device_id=peer, device_id_type=MESH)
        return copy

    barrier = pltpu.get_barrier_semaphore()
    pl.semaphore_signal(barrier, inc=1, device_id=mate, device_id_type=MESH)
    for i in range(1, rows):
        pl.semaphore_signal(barrier, inc=1, device_id=row_peer(i), device_id_type=MESH)
    for i in range(1, zs):
        pl.semaphore_signal(barrier, inc=1, device_id=z_peer(i), device_id_type=MESH)
    pl.semaphore_wait(barrier, rows + zs - 1)

    sent = []

    a_copies = []
    order = [k % rows for k in range(1, rows + 1)]
    for k in order:
        target = lax.rem(row + k, rows)
        copy = send(packed_ref.at[other, target], core_in.at[k], a_send.at[k], a_recv.at[k], mate)
        copy.start()
        a_copies.append(copy)
        sent.append(copy)
    b_copies = {}
    for k, arrived in zip(order, a_copies):
        arrived.wait_recv()
        target = lax.rem(row + k, rows)
        half[k] = packed_ref[core, target] + core_in[k]
        if k:
            for j in list(range(1, zs)) + [0]:
                spot = lax.rem(z + j, zs)
                copy = send(half.at[k, spot], row_in.at[k - 1, j], b_send.at[k - 1, j],
                            b_recv.at[k - 1, j], row_peer(k))
                copy.start()
                b_copies[k, j] = copy
                sent.append(copy)
    c_copies = []
    for j in list(range(1, zs)) + [0]:
        spot = lax.rem(z + j, zs)
        for k in range(1, rows):
            b_copies[k, j].wait_recv()
        total = half[0, spot]
        for k in range(1, rows):
            total = total + row_in[k - 1, j]
        part[j] = total
        if j:
            copy = send(part.at[j], z_in.at[j - 1], c_send.at[j - 1], c_recv.at[j - 1], z_peer(j))
            copy.start()
            c_copies.append(copy)
            sent.append(copy)
    for copy in c_copies:
        copy.wait_recv()
    total = part[0]
    for j in range(1, zs):
        total = total + z_in[j - 1]
    full[core, row, z] = total

    d_copies = []
    for j in range(1, zs):
        here = full.at[core, row, z]
        copy = send(here, here, d_send.at[j - 1], d_recv.at[j - 1], z_peer(j))
        copy.start()
        d_copies.append(copy)
        sent.append(copy)
    e_copies = {}
    f_copies = []
    for j in range(zs):
        spot = lax.rem(z + zs - j, zs)
        if j:
            d_copies[j - 1].wait_recv()
        here = full.at[core, row, spot]
        for k in range(1, rows):
            copy = send(here, here, e_send.at[k - 1, j], e_recv.at[k - 1, j], row_peer(k))
            copy.start()
            e_copies[k, j] = copy
            sent.append(copy)
    for k in range(rows):
        spot = lax.rem(row + rows - k, rows)
        if k:
            for j in range(zs):
                e_copies[k, j].wait_recv()
        here = full.at[core, spot]
        copy = send(here, here, f_send.at[k], f_recv.at[k], mate)
        copy.start()
        f_copies.append(copy)
        sent.append(copy)

    shard, width = momentum_ref.shape
    capacity = last_ref.shape[1]
    owner = row * (2 * zs) + col
    own_ids = owner * shard + lax.broadcasted_iota(jnp.int32, (shard, capacity), 0)
    slot_ids = lax.broadcasted_iota(jnp.int32, (shard, capacity), 1)
    picked = jnp.logical_and(own_ids == last_ref[...], slot_ids < count_ref[...])
    pick = jnp.where(picked, 1.0, 0.0).astype(jnp.bfloat16)

    for copy in f_copies:
        copy.wait_recv()
    scale = 1.0 / (rows * 2 * zs)
    piece = full.shape[3]
    per_lane = capacity // piece
    for lane in range(width // LANES):
        parts = []
        for p in range(lane * per_lane, (lane + 1) * per_lane):
            parts.append(full[p // (rows * zs), (p // zs) % rows, p % zs])
        total = jnp.concatenate(parts, axis=0) if per_lane > 1 else parts[0]
        high = total.astype(jnp.bfloat16)
        rest = total - high.astype(jnp.float32)
        middle = rest.astype(jnp.bfloat16)
        low = (rest - middle.astype(jnp.float32)).astype(jnp.bfloat16)
        rows_here = (jnp.dot(pick, high, preferred_element_type=jnp.float32)
                     + jnp.dot(pick, middle, preferred_element_type=jnp.float32)
                     + jnp.dot(pick, low, preferred_element_type=jnp.float32))
        lanes = slice(lane * LANES, (lane + 1) * LANES)
        out_ref[:, lanes] = decay_rate * momentum_ref[:, lanes] + rows_here * scale
    for copy in sent:
        copy.wait_send()


def sum_part(packed, momentum, last, count, rows, zs):
    width_lanes, capacity, _ = packed.shape
    pieces = 2 * rows * zs
    piece = width_lanes * capacity // pieces
    packed = packed.reshape(2, rows, zs, piece, LANES)
    vmem = pl.BlockSpec(memory_space=pltpu.VMEM)
    f32 = jnp.float32
    dma = pltpu.SemaphoreType.DMA
    return pl.pallas_call(
        functools.partial(sum_kernel, rows, zs),
        out_shape=jax.ShapeDtypeStruct(momentum.shape, f32),
        in_specs=[vmem] * 4,
        out_specs=vmem,
        scratch_shapes=[
            pltpu.VMEM((rows, zs, piece, LANES), f32),
            pltpu.VMEM((rows, zs, piece, LANES), f32),
            pltpu.VMEM((rows - 1, zs, piece, LANES), f32),
            pltpu.VMEM((zs, piece, LANES), f32),
            pltpu.VMEM((zs - 1, piece, LANES), f32),
            pltpu.VMEM((2, rows, zs, piece, LANES), f32),
            dma((rows,)), dma((rows,)),
            dma((rows - 1, zs)), dma((rows - 1, zs)),
            dma((zs - 1,)), dma((zs - 1,)),
            dma((zs - 1,)), dma((zs - 1,)),
            dma((rows - 1, zs)), dma((rows - 1, zs)),
            dma((rows,)), dma((rows,)),
        ],
        compiler_params=pltpu.CompilerParams(collective_id=0, has_side_effects=True),
        name="total",
    )(packed, momentum, last, count)


def body(tokens, grad_out, residual, momentum, kept_blocks, kept_counts):
    rows = lax.axis_size("row")
    zs = lax.axis_size("col") // 2
    lists = kept_blocks[0, 0]
    counts = kept_counts[0, 0]
    sections = lists.shape[0]
    residual_out, packed = local_part(tokens, grad_out, residual[0], lists, counts)
    momentum_out = sum_part(
        packed, momentum, lists[sections - 1:], counts[sections - 1:].reshape(1, 1), rows, zs)
    return (residual_out[None], momentum_out)


def solution(mesh):
    in_specs = (
        P(("row", "col"), None),
        P(("row", "col"), None),
        P(("row", "col"), None, None),
        P(("row", "col"), None),
        P("row", "col", None, None),
        P("row", "col", None),
    )
    out_specs = (P(("row", "col"), None, None), P(("row", "col"), None))
    return jax.shard_map(body, mesh=mesh, in_specs=in_specs, out_specs=out_specs, check_vma=False)
```

time: 104 us -> 43.5 us (0.42)
  waiting for transfers between devices: 40.6 us -> 0 us
  Pallas kernels: 0 us -> 36.7 us
  local copies, waits for them, and re-layouts: 25.9 us -> 5.45 us
  other arithmetic: 18.6 us -> 0 us
  starting transfers between devices: 9.16 us -> 0 us
  matrix products: 8.23 us -> 0 us
    ppermute x5 -> x0, waiting for transfers between devices: 40.6 us -> none  [partner(): return lax.ppermute(value, axis, pairs)]
    pallas_call x0 -> x2, Pallas kernels: none -> 36.7 us  [the longest x1 26.2 us: sum_part(): pl.pallas_call(functools.partial(sum_kernel, rows, zs), out_shape=jax.Sha...]
    reshape x2 -> x0, local copies, waits for them, and re-layouts: 19.8 us -> none  [body(): weight_grad.reshape(block_count, block_width)]
    add x2 -> x0, other arithmetic: 9.99 us -> none  [the longest x1 9.98 us: body(): weight_grad.reshape(block_count, block_width)]
    ppermute x5 -> x0, starting transfers between devices: 9.16 us -> none  [partner(): return lax.ppermute(value, axis, pairs)]
    dot_general x6 -> x0, matrix products: 8.23 us -> none  [the longest x1 5.47 us: body(): lax.dot_general(tokens, grad_out, (((0,), (0,)), ((), ())), preferred_ele...]
    convert_element_type x2 -> x0, other arithmetic: 7.16 us -> none  [the longest x1 7.15 us: body(): jnp.where(kept_mask[:, None], 0.0, accumulated).astype(jnp.bfloat16)[None]]
    gather x1 -> x0, local copies, waits for them, and re-layouts: 4.42 us -> none  [body(): accumulated[block_lists[0]] * is_valid[0][:, None].astype(jnp.float32)]
  transfers between devices with their start and end apart: 5 -> 0, of which waited for: 5 -> 0; matrix products, arithmetic and copies ran while one was open for 18% -> 0% of each run, Pallas kernels for 0% -> 0%
where the time goes in v1:
time: 43.5 us; the launch traced here: 42.8 us
  Pallas kernels  36.7 us (84%)
  local copies, waits for them, and re-layouts  5.45 us (13%)
  between operations  0.64 us (1%)
    pallas_call x1, Pallas kernels, sum_part(): pl.pallas_call(functools.partial(sum_kernel, rows, zs), out_shape=jax.Sha...  26.2 us
    pallas_call x1, Pallas kernels, local_part(): pl.pallas_call(functools.partial(local_kernel, steps), grid_spec=pltpu.Pr...  10.6 us
    unnamed x2, local copies, waits for them, and re-layouts  2.95 us
    slice x1, local copies, waits for them, and re-layouts, body(): counts[sections - 1:].reshape(1, 1)  1.26 us
    slice x1, local copies, waits for them, and re-layouts, local_part(): lists[sections - 1]  1.24 us

profile of v1, /device:TPU:0, one launch (start us, length us, event | category | flops | bytes accessed | tf_op | source)
XLA Modules:
  0.0 42.8 jit_solution(5760505907777562716)
XLA Ops:
  0.6 1.3 %slice.13 = s32[1,1,1]{2,1,0:T(1,128)} slice(s32[1,1,5]{2,1,0:T(1,128)} %param.11), slice={[0:1], [0:1], [4:5]} | slice | bytes 8 | tf_op jit(solution)/shard_map/slice | solution.py:289
  1.9 1.2 %slice_bitcast_fusion = (s32[1,128]{1,0:T(1,128)}, s32[128]{0:T(128)}) fusion(s32[1,1,5,128]{3,1,2,0:T(1,128)} %param.10), kind=kLoop, calls=%fused_computation.1 | loop fusion | bytes 1536 | tf_op jit(solution)/shard_map/slice | solution.py:110
  3.1 1.3 %copy.10 = s32[1,1,5,128]{3,2,1,0:T(8,128)} copy(s32[1,1,5,128]{3,1,2,0:T(1,128)} %param.10) | data formatting | bytes 5120
  4.4 10.6 %local.1 = (bf16[2048,1024]{1,0:T(8,128)(2,1)}, f32[8,128,128]{2,1,0:T(8,128)}) custom-call(s32[128]{0:T(128)} %get-tuple-element.7.last_ref, bf16[256,4096]{1,0:T(8,128)(2,1)} %tokens_ref.1, bf16[256,512]{1,0:T(8,128)(2,1)} %grad_ref.1, bf16[2048,1024]{1,0:T(8,128)(2,1)} %bitcast.12, s32[5,128]{1,0:T(8,128)} %bitcast.14, s32[5]{0:T(128)} %bitcast.15), custom_call_target="tpu_custom_call" | custom-call | tf_op jit(solution)/shard_map/local/pallas_call | solution.py:82
  15.0 26.2 %total.1 = f32[64,1024]{1,0:T(8,128)} custom-call(f32[2,4,4,32,128]{4,3,2,1,0:T(8,128)} %bitcast.13, f32[64,1024]{1,0:T(8,128)} %momentum_ref.1, s32[1,128]{1,0:T(1,128)} %get-tuple-element.6.last_ref, s32[1,1]{1,0:T(1,128)} %bitcast.6.count_ref), custom_call_target="tpu_custom_call" | custom-call | tf_op jit(solution)/shard_map/total/pallas_call | solution.py:257
  41.1 1.7 %copy.12 = f32[64,1024]{1,0:T(8,128)} copy(f32[64,1024]{1,0:T(8,128)} %total.1) | data formatting | bytes 524288

commit v2 on v0

v2 whole, which is shorter than its diff:
```python
import functools

import jax
import jax.numpy as jnp
from jax import lax
from jax.experimental import pallas as pl
from jax.experimental.pallas import tpu as pltpu
from jax.sharding import PartitionSpec as P

decay_rate = 0.9
MESH = pl.DeviceIdType.MESH
LANES = 128


def column_of(row):
    n = row.shape[1]
    down = lax.broadcasted_iota(jnp.int32, (n, n), 0)
    along = lax.broadcasted_iota(jnp.int32, (n, n), 1)
    spread = jnp.broadcast_to(row, (n, n))
    return jnp.sum(jnp.where(down == along, spread, 0), axis=1, keepdims=True)


def local_kernel(chunk, tokens_hbm, grad_hbm, residual_hbm, lists_ref, list_ids_hbm, counts_ref,
                 out_hbm, packed_ref, tokens, grad, values, acc, gathered, list_ids,
                 token_sems, value_sems, out_sems, grad_sem, list_sem):
    blocks = values.shape[0]
    half = grad.shape[1]
    sections, _, capacity = lists_ref.shape
    steps = blocks // chunk

    def spans(step):
        return slice(step * chunk, (step + 1) * chunk), slice(2 * step * chunk, 2 * (step + 1) * chunk)

    grad_copy = pltpu.make_async_copy(grad_hbm, grad, grad_sem)
    grad_copy.start()
    list_copy = pltpu.make_async_copy(list_ids_hbm, list_ids, list_sem)
    list_copy.start()
    copies = []
    for step in range(steps):
        rows, columns = spans(step)
        token_copy = pltpu.make_async_copy(tokens_hbm.at[:, columns], tokens.at[:, columns], token_sems.at[step])
        value_copy = pltpu.make_async_copy(residual_hbm.at[rows], values.at[rows], value_sems.at[step])
        token_copy.start()
        value_copy.start()
        copies.append((token_copy, value_copy))

    slot_ids = lax.broadcasted_iota(jnp.int32, (1, capacity), 1)
    last = lists_ref[sections - 1]
    kept = jnp.where(slot_ids < counts_ref[sections - 1], 1, 0)
    for section in range(sections - 1):
        row = jnp.where(slot_ids < counts_ref[section], lists_ref[section], -1)
        hits = jnp.where(column_of(row) == last, 1, 0)
        kept = kept * jnp.max(hits, axis=0, keepdims=True)
    marks = jnp.where(kept > 0, last, -1)
    keep_slot = column_of(marks) >= 0

    sub = 256
    out_ids = lax.broadcasted_iota(jnp.int32, (sub, sub), 0)
    in_ids = lax.broadcasted_iota(jnp.int32, (sub, sub), 1)
    source = jnp.where(out_ids < sub // 2, 2 * out_ids, 2 * out_ids - sub + 1)
    shuffle = (source == in_ids).astype(jnp.float32).astype(jnp.bfloat16)
    grad_copy.wait()
    out_copies = []
    for step in range(steps):
        for copy in copies[step]:
            copy.wait()
        for piece in range(2 * chunk // sub):
            start = step * chunk + piece * (sub // 2)
            rows = slice(start, start + sub // 2)
            turned = lax.dot_general(
                shuffle, tokens[:, 2 * start:2 * start + sub], (((1,), (1,)), ((), ())),
                preferred_element_type=jnp.float32,
            ).astype(jnp.bfloat16)
            grads = jnp.dot(turned, grad[...], preferred_element_type=jnp.float32)
            block_ids = start + lax.broadcasted_iota(jnp.int32, (sub // 2, capacity), 0)
            kept_row = jnp.max(jnp.where(block_ids == marks, 1, 0), axis=1, keepdims=True) > 0
            for side in range(2):
                columns = slice(side * half, (side + 1) * half)
                total = grads[side * (sub // 2):(side + 1) * (sub // 2)] + values[rows, columns].astype(jnp.float32)
                acc[rows, columns] = total
                values[rows, columns] = jnp.where(kept_row, 0.0, total).astype(jnp.bfloat16)
        rows, _ = spans(step)
        copy = pltpu.make_async_copy(values.at[rows], out_hbm.at[rows], out_sems.at[step])
        copy.start()
        out_copies.append(copy)

    list_copy.wait()

    def fetch(slot, carry):
        gathered[pl.ds(slot, 1), :] = acc[pl.ds(list_ids[sections - 1, 0, slot], 1), :]
        return carry

    lax.fori_loop(0, capacity, fetch, 0, unroll=8)
    for lane in range(packed_ref.shape[0]):
        packed_ref[lane] = jnp.where(keep_slot, gathered[:, lane * LANES:(lane + 1) * LANES], 0.0)
    for copy in out_copies:
        copy.wait()


def local_part(tokens, grad_out, residual, lists, counts):
    token_count, features = tokens.shape
    half = grad_out.shape[1]
    blocks, width = residual.shape
    sections, _, capacity = lists.shape
    chunk = 256
    steps = blocks // chunk
    hbm = pl.BlockSpec(memory_space=pl.ANY)
    dma = pltpu.SemaphoreType.DMA
    return pl.pallas_call(
        functools.partial(local_kernel, chunk),
        in_specs=[
            hbm, hbm, hbm,
            pl.BlockSpec(memory_space=pltpu.VMEM),
            hbm,
            pl.BlockSpec(memory_space=pltpu.SMEM),
        ],
        out_specs=[hbm, pl.BlockSpec(memory_space=pltpu.VMEM)],
        scratch_shapes=[
            pltpu.VMEM((token_count, features), jnp.bfloat16),
            pltpu.VMEM((token_count, half), jnp.bfloat16),
            pltpu.VMEM((blocks, width), jnp.bfloat16),
            pltpu.VMEM((blocks, width), jnp.float32),
            pltpu.VMEM((capacity, width), jnp.float32),
            pltpu.SMEM((sections, 1, capacity), jnp.int32),
            dma((steps,)), dma((steps,)), dma((steps,)), dma(()), dma(()),
        ],
        out_shape=[
            jax.ShapeDtypeStruct((blocks, width), jnp.bfloat16),
            jax.ShapeDtypeStruct((width // LANES, capacity, LANES), jnp.float32),
        ],
        name="local",
    )(tokens, grad_out, residual, lists, lists, counts)


def sum_kernel(rows, zs, shard, packed_ref, lists_ref, counts_ref, out_ref,
               own, core_in, half, row_in, part, z_in, full,
               own_sem, a_send, a_recv, b_send, b_recv, c_send, c_recv,
               d_send, d_recv, e_send, e_recv, f_send, f_recv):
    row = lax.axis_index("row")
    col = lax.axis_index("col")
    z = col // 2
    core = col % 2
    other = 1 - core
    mate = (row, z * 2 + other)

    def row_peer(k):
        return (lax.rem(row + k, rows), col)

    def z_peer(j):
        return (row, lax.rem(z + j, zs) * 2 + core)

    sent = []

    def send(src, dst, send_sem, recv_sem, peer):
        copy = pltpu.make_async_remote_copy(
            src_ref=src, dst_ref=dst, send_sem=send_sem, recv_sem=recv_sem,
            device_id=peer, device_id_type=MESH)
        copy.start()
        sent.append(copy)
        return copy

    own_copy = pltpu.make_async_copy(packed_ref.at[core], own, own_sem)
    own_copy.start()
    barrier = pltpu.get_barrier_semaphore()
    pl.semaphore_signal(barrier, inc=1, device_id=mate, device_id_type=MESH)
    for k in range(1, rows):
        pl.semaphore_signal(barrier, inc=1, device_id=row_peer(k), device_id_type=MESH)
    for j in range(1, zs):
        pl.semaphore_signal(barrier, inc=1, device_id=z_peer(j), device_id_type=MESH)
    pl.semaphore_wait(barrier, rows + zs - 1)

    order = [j % zs for j in range(1, zs + 1)]
    a_copies = {}
    for j in order:
        spot = lax.rem(z + j, zs)
        a_copies[j] = send(packed_ref.at[other, spot], core_in.at[j], a_send.at[j], a_recv.at[j], mate)
    own_copy.wait()
    b_copies = {}
    for j in order:
        a_copies[j].wait_recv()
        half[j] = own[lax.rem(z + j, zs)] + core_in[j]
        for k in range(1, rows):
            b_copies[j, k] = send(half.at[j, lax.rem(row + k, rows)], row_in.at[j, k - 1],
                                  b_send.at[j, k - 1], b_recv.at[j, k - 1], row_peer(k))
    c_copies = []
    for j in order:
        for k in range(1, rows):
            b_copies[j, k].wait_recv()
        total = half[j, row]
        for k in range(1, rows):
            total = total + row_in[j, k - 1]
        part[j] = total
        if j:
            c_copies.append(send(part.at[j], z_in.at[j - 1], c_send.at[j - 1], c_recv.at[j - 1], z_peer(j)))
    total = part[0]
    for j, copy in enumerate(c_copies):
        copy.wait_recv()
        total = total + z_in[j]
    full[core, z, row] = total

    d_copies = {}
    for j in range(1, zs):
        here = full.at[core, z, row]
        d_copies[j] = send(here, here, d_send.at[j - 1], d_recv.at[j - 1], z_peer(j))
    e_copies = {}
    f_copies = {}

    def back_to_core(j):
        for k in range(1, rows):
            e_copies[j, k].wait_recv()
        here = full.at[core, lax.rem(z + zs - j, zs)]
        f_copies[j] = send(here, here, f_send.at[j], f_recv.at[j], mate)

    for j in range(zs):
        if j:
            d_copies[j].wait_recv()
        here = full.at[core, lax.rem(z + zs - j, zs), row]
        for k in range(1, rows):
            e_copies[j, k] = send(here, here, e_send.at[j, k - 1], e_recv.at[j, k - 1], row_peer(k))
        if j >= 2:
            back_to_core(j - 2)
    for j in range(max(zs - 2, 0), zs):
        back_to_core(j)

    sections, _, capacity = lists_ref.shape
    owner = row * (2 * zs) + col
    own_ids = owner * shard + lax.broadcasted_iota(jnp.int32, (shard, capacity), 0)
    slot_ids = lax.broadcasted_iota(jnp.int32, (shard, capacity), 1)
    picked = jnp.logical_and(own_ids == lists_ref[sections - 1], slot_ids < counts_ref[sections - 1])
    pick = jnp.where(picked, 1.0, 0.0).astype(jnp.bfloat16)
    lane_groups = out_ref.shape[1] // LANES // 2
    slabs = zs // lane_groups

    def emit(side):
        for lane in range(lane_groups):
            parts = [full[side, slab, r] for slab in range(lane * slabs, (lane + 1) * slabs) for r in range(rows)]
            total = jnp.concatenate(parts, axis=0)
            high = total.astype(jnp.bfloat16)
            rest = total - high.astype(jnp.float32)
            middle = rest.astype(jnp.bfloat16)
            low = (rest - middle.astype(jnp.float32)).astype(jnp.bfloat16)
            rows_here = (jnp.dot(pick, high, preferred_element_type=jnp.float32)
                         + jnp.dot(pick, middle, preferred_element_type=jnp.float32)
                         + jnp.dot(pick, low, preferred_element_type=jnp.float32))
            lanes = pl.ds(pl.multiple_of((side * lane_groups + lane) * LANES, LANES), LANES)
            out_ref[:, lanes] = rows_here

    emit(core)
    for j in range(zs):
        f_copies[j].wait_recv()
    emit(other)
    for copy in sent:
        copy.wait_send()


def sum_part(packed, shard, lists, counts, rows, zs):
    width_lanes, capacity, _ = packed.shape
    piece = width_lanes * capacity // (2 * rows * zs)
    packed = packed.reshape(2, zs, rows, piece, LANES)
    vmem = pl.BlockSpec(memory_space=pltpu.VMEM)
    f32 = jnp.float32
    dma = pltpu.SemaphoreType.DMA
    return pl.pallas_call(
        functools.partial(sum_kernel, rows, zs, shard),
        out_shape=jax.ShapeDtypeStruct((shard, width_lanes * LANES), f32),
        in_specs=[pl.BlockSpec(memory_space=pl.ANY), vmem, pl.BlockSpec(memory_space=pltpu.SMEM)],
        out_specs=vmem,
        scratch_shapes=[
            pltpu.VMEM((zs, rows, piece, LANES), f32),
            pltpu.VMEM((zs, rows, piece, LANES), f32),
            pltpu.VMEM((zs, rows, piece, LANES), f32),
            pltpu.VMEM((zs, rows - 1, piece, LANES), f32),
            pltpu.VMEM((zs, piece, LANES), f32),
            pltpu.VMEM((zs - 1, piece, LANES), f32),
            pltpu.VMEM((2, zs, rows, piece, LANES), f32),
            dma(()),
            dma((zs,)), dma((zs,)),
            dma((zs, rows - 1)), dma((zs, rows - 1)),
            dma((zs - 1,)), dma((zs - 1,)),
            dma((zs - 1,)), dma((zs - 1,)),
            dma((zs, rows - 1)), dma((zs, rows - 1)),
            dma((zs,)), dma((zs,)),
        ],
        compiler_params=pltpu.CompilerParams(collective_id=0, has_side_effects=True),
        name="total",
    )(packed, lists, counts)


def body(tokens, grad_out, residual, momentum, kept_blocks, kept_counts):
    rows = lax.axis_size("row")
    zs = lax.axis_size("col") // 2
    sections, capacity = kept_blocks.shape[2:]
    lists = kept_blocks.reshape(sections, 1, capacity)
    counts = kept_counts.reshape(sections)
    residual_out, packed = local_part(tokens, grad_out, residual[0], lists, counts)
    total_shard = sum_part(packed, momentum.shape[0], lists, counts, rows, zs)
    momentum_out = decay_rate * momentum + total_shard / (rows * 2 * zs)
    return (residual_out[None], momentum_out)


def solution(mesh):
    in_specs = (
        P(("row", "col"), None),
        P(("row", "col"), None),
        P(("row", "col"), None, None),
        P(("row", "col"), None),
        P("row", "col", None, None),
        P("row", "col", None),
    )
    out_specs = (P(("row", "col"), None, None), P(("row", "col"), None))
    return jax.shard_map(body, mesh=mesh, in_specs=in_specs, out_specs=out_specs, check_vma=False)
```

time: 104 us -> 37.4 us (0.36)
  waiting for transfers between devices: 40.6 us -> 0 us
  Pallas kernels: 0 us -> 34.7 us
  local copies, waits for them, and re-layouts: 25.9 us -> 0.01 us
  other arithmetic: 18.6 us -> 1.69 us
  starting transfers between devices: 9.16 us -> 0 us
  matrix products: 8.23 us -> 0 us
    ppermute x5 -> x0, waiting for transfers between devices: 40.6 us -> none  [partner(): return lax.ppermute(value, axis, pairs)]
    pallas_call x0 -> x2, Pallas kernels: none -> 34.7 us  [the longest x1 25.1 us: sum_part(): pl.pallas_call(functools.partial(sum_kernel, rows, zs, shard), out_shape=...]
    reshape x2 -> x0, local copies, waits for them, and re-layouts: 19.8 us -> none  [body(): weight_grad.reshape(block_count, block_width)]
    ppermute x5 -> x0, starting transfers between devices: 9.16 us -> none  [partner(): return lax.ppermute(value, axis, pairs)]
    add x2 -> x1, other arithmetic: 9.99 us -> 1.69 us  [body(): momentum_out = decay_rate * momentum + total_shard / (rows * 2 * zs)]
    dot_general x6 -> x0, matrix products: 8.23 us -> none  [the longest x1 5.47 us: body(): lax.dot_general(tokens, grad_out, (((0,), (0,)), ((), ())), preferred_ele...]
    convert_element_type x2 -> x0, other arithmetic: 7.16 us -> none  [the longest x1 7.15 us: body(): jnp.where(kept_mask[:, None], 0.0, accumulated).astype(jnp.bfloat16)[None]]
    gather x1 -> x0, local copies, waits for them, and re-layouts: 4.42 us -> none  [body(): accumulated[block_lists[0]] * is_valid[0][:, None].astype(jnp.float32)]
  transfers between devices with their start and end apart: 5 -> 0, of which waited for: 5 -> 0; matrix products, arithmetic and copies ran while one was open for 18% -> 0% of each run, Pallas kernels for 0% -> 0%
where the time goes in v2:
time: 37.4 us; the launch traced here: 37.1 us
  Pallas kernels  34.7 us (93%)
  other arithmetic  1.69 us (5%)
  between operations  0.66 us (2%)
    pallas_call x1, Pallas kernels, sum_part(): pl.pallas_call(functools.partial(sum_kernel, rows, zs, shard), out_shape=...  25.1 us
    pallas_call x1, Pallas kernels, local_part(): pl.pallas_call(functools.partial(local_kernel, chunk), in_specs=[hbm, hbm...  9.6 us
    add x1, other arithmetic, body(): momentum_out = decay_rate * momentum + total_shard / (rows * 2 * zs)  1.69 us

profile of v2, /device:TPU:0, one launch (start us, length us, event | category | flops | bytes accessed | tf_op | source)
XLA Modules:
  0.0 37.1 jit_solution(7802539909669289048)
XLA Ops:
  0.6 0.0 copy-start
  0.6 9.6 %local.1 = (bf16[2048,1024]{1,0:T(8,128)(2,1)}, f32[8,128,128]{2,1,0:T(8,128)}) custom-call(bf16[256,4096]{1,0:T(8,128)(2,1)} %tokens_hbm.1, bf16[256,512]{1,0:T(8,128)(2,1)} %grad_hbm.1, bf16[2048,1024]{1,0:T(8,128)(2,1)} %bitcast.5, s32[5,1,128]{2,1,0:T(1,128)} %bitcast.7, s32[5,1,128]{2,1,0:T(1,128)} %bitcast.8, s32[5]{0:T(128)} %bitcast.10), custom_call_target="tpu_custom_call" | custom-call | tf_op jit(solution)/shard_map/local/pallas_call | solution.py:109
  10.2 25.1 %total.1 = f32[64,1024]{1,0:T(8,128)} custom-call(f32[2,4,4,32,128]{4,3,2,1,0:T(8,128)} %bitcast.6, s32[5,1,128]{2,1,0:T(1,128)} %bitcast.9, s32[5]{0:T(128)} %bitcast.11), custom_call_target="tpu_custom_call" | custom-call | tf_op jit(solution)/shard_map/total/pallas_call | solution.py:263
  35.4 0.0 copy-done
  35.4 1.7 %multiply_add_fusion = f32[64,1024]{1,0:T(8,128)} fusion(f32[64,1024]{1,0:T(8,128)} %total.1, f32[64,1024]{1,0:T(8,128)S(1)} %copy-done), kind=kLoop, calls=%fused_computation | loop fusion | flops 196608 | bytes 786432 | tf_op jit(solution)/shard_map/add | solution.py:297
Async XLA Ops:
  0.6 34.7 %copy-start = (f32[64,1024]{1,0:T(8,128)S(1)}, f32[64,1024]{1,0:T(8,128)}, u32[]{:S(2)}) copy-start(f32[64,1024]{1,0:T(8,128)} %param.9) | copy-start | bytes 786436

commit v3 on v2

--- a/solution.py
+++ b/solution.py
@@ -21,7 +21,7 @@
 
 
 def local_kernel(chunk, tokens_hbm, grad_hbm, residual_hbm, lists_ref, list_ids_hbm, counts_ref,
-                 out_hbm, packed_ref, tokens, grad, values, acc, gathered, list_ids,
+                 out_hbm, packed_ref, tokens, grad, values, turned, acc, gathered, list_ids,
                  token_sems, value_sems, out_sems, grad_sem, list_sem):
     blocks = values.shape[0]
     half = grad.shape[1]
@@ -35,14 +35,17 @@
     grad_copy.start()
     list_copy = pltpu.make_async_copy(list_ids_hbm, list_ids, list_sem)
     list_copy.start()
-    copies = []
+    token_copies = []
+    value_copies = []
     for step in range(steps):
         rows, columns = spans(step)
-        token_copy = pltpu.make_async_copy(tokens_hbm.at[:, columns], tokens.at[:, columns], token_sems.at[step])
-        value_copy = pltpu.make_async_copy(residual_hbm.at[rows], values.at[rows], value_sems.at[step])
-        token_copy.start()
-        value_copy.start()
-        copies.append((token_copy, value_copy))
+        token_copies.append(pltpu.make_async_copy(tokens_hbm.at[:, columns], tokens.at[:, columns], token_sems.at[step]))
+        value_copies.append(pltpu.make_async_copy(residual_hbm.at[rows], values.at[rows], value_sems.at[step]))
+    token_copies[0].start()
+    for step in range(steps):
+        if step + 1 < steps:
+            token_copies[step + 1].start()
+        value_copies[step].start()
 
     slot_ids = lax.broadcasted_iota(jnp.int32, (1, capacity), 1)
     last = lists_ref[sections - 1]
@@ -59,19 +62,29 @@
     in_ids = lax.broadcasted_iota(jnp.int32, (sub, sub), 1)
     source = jnp.where(out_ids < sub // 2, 2 * out_ids, 2 * out_ids - sub + 1)
     shuffle = (source == in_ids).astype(jnp.float32).astype(jnp.bfloat16)
+    pieces = 2 * chunk // sub
+    out_copies = []
+
+    def turn(step, piece):
+        columns = slice((step * pieces + piece) * sub, (step * pieces + piece + 1) * sub)
+        turned[columns, :] = lax.dot_general(
+            shuffle, tokens[:, columns], (((1,), (1,)), ((), ())), preferred_element_type=jnp.float32
+        ).astype(jnp.bfloat16)
+
+    token_copies[0].wait()
+    for piece in range(pieces):
+        turn(0, piece)
     grad_copy.wait()
-    out_copies = []
     for step in range(steps):
-        for copy in copies[step]:
-            copy.wait()
-        for piece in range(2 * chunk // sub):
+        value_copies[step].wait()
+        if step + 1 < steps:
+            token_copies[step + 1].wait()
+        for piece in range(pieces):
+            if step + 1 < steps:
+                turn(step + 1, piece)
             start = step * chunk + piece * (sub // 2)
             rows = slice(start, start + sub // 2)
-            turned = lax.dot_general(
-                shuffle, tokens[:, 2 * start:2 * start + sub], (((1,), (1,)), ((), ())),
-                preferred_element_type=jnp.float32,
-            ).astype(jnp.bfloat16)
-            grads = jnp.dot(turned, grad[...], preferred_element_type=jnp.float32)
+            grads = jnp.dot(turned[2 * start:2 * start + sub, :], grad[...], preferred_element_type=jnp.float32)
             block_ids = start + lax.broadcasted_iota(jnp.int32, (sub // 2, capacity), 0)
             kept_row = jnp.max(jnp.where(block_ids == marks, 1, 0), axis=1, keepdims=True) > 0
             for side in range(2):
@@ -102,7 +115,7 @@
     half = grad_out.shape[1]
     blocks, width = residual.shape
     sections, _, capacity = lists.shape
-    chunk = 256
+    chunk = 512
     steps = blocks // chunk
     hbm = pl.BlockSpec(memory_space=pl.ANY)
     dma = pltpu.SemaphoreType.DMA
@@ -119,6 +132,7 @@
             pltpu.VMEM((token_count, features), jnp.bfloat16),
             pltpu.VMEM((token_count, half), jnp.bfloat16),
             pltpu.VMEM((blocks, width), jnp.bfloat16),
+            pltpu.VMEM((features, token_count), jnp.bfloat16),
             pltpu.VMEM((blocks, width), jnp.float32),
             pltpu.VMEM((capacity, width), jnp.float32),
             pltpu.SMEM((sections, 1, capacity), jnp.int32),

time: 37.4 us -> 35.2 us (0.941)
  Pallas kernels: 34.7 us -> 32.5 us
    pallas_call x1, Pallas kernels: 9.6 us -> 7.39 us  [local_part(): pl.pallas_call(functools.partial(local_kernel, chunk), in_specs=[hbm, hbm...]
where the time goes in v3:
time: 35.2 us; the launch traced here: 34.9 us
  Pallas kernels  32.5 us (92%)
  other arithmetic  1.69 us (5%)
  between operations  0.66 us (2%)
    pallas_call x1, Pallas kernels, sum_part(): pl.pallas_call(functools.partial(sum_kernel, rows, zs, shard), out_shape=...  25.1 us
    pallas_call x1, Pallas kernels, local_part(): pl.pallas_call(functools.partial(local_kernel, chunk), in_specs=[hbm, hbm...  7.39 us
    add x1, other arithmetic, body(): momentum_out = decay_rate * momentum + total_shard / (rows * 2 * zs)  1.69 us

profile of v3, /device:TPU:0, one launch (start us, length us, event | category | flops | bytes accessed | tf_op | source)
XLA Modules:
  0.0 34.9 jit_solution(17362970524298795345)
XLA Ops:
  0.6 0.0 copy-start
  0.6 7.4 %local.1 = (bf16[2048,1024]{1,0:T(8,128)(2,1)}, f32[8,128,128]{2,1,0:T(8,128)}) custom-call(bf16[256,4096]{1,0:T(8,128)(2,1)} %tokens_hbm.1, bf16[256,512]{1,0:T(8,128)(2,1)} %grad_hbm.1, bf16[2048,1024]{1,0:T(8,128)(2,1)} %bitcast.5, s32[5,1,128]{2,1,0:T(1,128)} %bitcast.7, s32[5,1,128]{2,1,0:T(1,128)} %bitcast.8, s32[5]{0:T(128)} %bitcast.10), custom_call_target="tpu_custom_call" | custom-call | tf_op jit(solution)/shard_map/local/pallas_call | solution.py:122
  8.0 25.1 %total.1 = f32[64,1024]{1,0:T(8,128)} custom-call(f32[2,4,4,32,128]{4,3,2,1,0:T(8,128)} %bitcast.6, s32[5,1,128]{2,1,0:T(1,128)} %bitcast.9, s32[5]{0:T(128)} %bitcast.11), custom_call_target="tpu_custom_call" | custom-call | tf_op jit(solution)/shard_map/total/pallas_call | solution.py:277
  33.2 0.0 copy-done
  33.2 1.7 %multiply_add_fusion = f32[64,1024]{1,0:T(8,128)} fusion(f32[64,1024]{1,0:T(8,128)} %total.1, f32[64,1024]{1,0:T(8,128)S(1)} %copy-done), kind=kLoop, calls=%fused_computation | loop fusion | flops 196608 | bytes 786432 | tf_op jit(solution)/shard_map/add | solution.py:311
Async XLA Ops:
  0.6 32.6 %copy-start = (f32[64,1024]{1,0:T(8,128)S(1)}, f32[64,1024]{1,0:T(8,128)}, u32[]{:S(2)}) copy-start(f32[64,1024]{1,0:T(8,128)} %param.9) | copy-start | bytes 786436

commit v4 on v3

--- a/solution.py
+++ b/solution.py
@@ -18,6 +18,13 @@
     along = lax.broadcasted_iota(jnp.int32, (n, n), 1)
     spread = jnp.broadcast_to(row, (n, n))
     return jnp.sum(jnp.where(down == along, spread, 0), axis=1, keepdims=True)
+
+
+def flipped(index, mask):
+    for bit in range(mask.bit_length()):
+        if mask >> bit & 1:
+            index = index + 2**bit * (1 - 2 * (index // 2**bit % 2))
+    return index
 
 
 def local_kernel(chunk, tokens_hbm, grad_hbm, residual_hbm, lists_ref, list_ids_hbm, counts_ref,
@@ -140,7 +147,7 @@
         ],
         out_shape=[
             jax.ShapeDtypeStruct((blocks, width), jnp.bfloat16),
-            jax.ShapeDtypeStruct((width // LANES, capacity, LANES), jnp.float32),
+            pltpu.VMEM((width // LANES, capacity, LANES), jnp.float32),
         ],
         name="local",
     )(tokens, grad_out, residual, lists, lists, counts)
@@ -158,10 +165,10 @@
     mate = (row, z * 2 + other)
 
     def row_peer(k):
-        return (lax.rem(row + k, rows), col)
+        return (flipped(row, k), col)
 
     def z_peer(j):
-        return (row, lax.rem(z + j, zs) * 2 + core)
+        return (row, flipped(z, j) * 2 + core)
 
     sent = []
 
@@ -183,20 +190,21 @@
         pl.semaphore_signal(barrier, inc=1, device_id=z_peer(j), device_id_type=MESH)
     pl.semaphore_wait(barrier, rows + zs - 1)
 
-    order = [j % zs for j in range(1, zs + 1)]
+    order = list(range(zs - 1, -1, -1))
+    far_rows = list(range(rows - 1, 0, -1))
     a_copies = {}
     for j in order:
-        spot = lax.rem(z + j, zs)
+        spot = flipped(z, j)
         a_copies[j] = send(packed_ref.at[other, spot], core_in.at[j], a_send.at[j], a_recv.at[j], mate)
     own_copy.wait()
     b_copies = {}
     for j in order:
         a_copies[j].wait_recv()
-        half[j] = own[lax.rem(z + j, zs)] + core_in[j]
-        for k in range(1, rows):
-            b_copies[j, k] = send(half.at[j, lax.rem(row + k, rows)], row_in.at[j, k - 1],
+        half[j] = own[flipped(z, j)] + core_in[j]
+        for k in far_rows:
+            b_copies[j, k] = send(half.at[j, flipped(row, k)], row_in.at[j, k - 1],
                                   b_send.at[j, k - 1], b_recv.at[j, k - 1], row_peer(k))
-    c_copies = []
+    c_copies = {}
     for j in order:
         for k in range(1, rows):
             b_copies[j, k].wait_recv()
@@ -205,36 +213,12 @@
             total = total + row_in[j, k - 1]
         part[j] = total
         if j:
-            c_copies.append(send(part.at[j], z_in.at[j - 1], c_send.at[j - 1], c_recv.at[j - 1], z_peer(j)))
+            c_copies[j] = send(part.at[j], z_in.at[j - 1], c_send.at[j - 1], c_recv.at[j - 1], z_peer(j))
     total = part[0]
-    for j, copy in enumerate(c_copies):
-        copy.wait_recv()
-        total = total + z_in[j]
+    for j in range(1, zs):
+        c_copies[j].wait_recv()
+        total = total + z_in[j - 1]
     full[core, z, row] = total
-
-    d_copies = {}
-    for j in range(1, zs):
-        here = full.at[core, z, row]
-        d_copies[j] = send(here, here, d_send.at[j - 1], d_recv.at[j - 1], z_peer(j))
-    e_copies = {}
-    f_copies = {}
-
-    def back_to_core(j):
-        for k in range(1, rows):
-            e_copies[j, k].wait_recv()
-        here = full.at[core, lax.rem(z + zs - j, zs)]
-        f_copies[j] = send(here, here, f_send.at[j], f_recv.at[j], mate)
-
-    for j in range(zs):
-        if j:
-            d_copies[j].wait_recv()
-        here = full.at[core, lax.rem(z + zs - j, zs), row]
-        for k in range(1, rows):
-            e_copies[j, k] = send(here, here, e_send.at[j, k - 1], e_recv.at[j, k - 1], row_peer(k))
-        if j >= 2:
-            back_to_core(j - 2)
-    for j in range(max(zs - 2, 0), zs):
-        back_to_core(j)
 
     sections, _, capacity = lists_ref.shape
     owner = row * (2 * zs) + col
@@ -245,24 +229,55 @@
     lane_groups = out_ref.shape[1] // LANES // 2
     slabs = zs // lane_groups
 
-    def emit(side):
+    def emit_lane(side, lane):
+        parts = [full[side, lane * slabs + slab, r] for slab in range(slabs) for r in range(rows)]
+        total = jnp.concatenate(parts, axis=0)
+        high = total.astype(jnp.bfloat16)
+        rest = total - high.astype(jnp.float32)
+        middle = rest.astype(jnp.bfloat16)
+        low = (rest - middle.astype(jnp.float32)).astype(jnp.bfloat16)
+        rows_here = (jnp.dot(pick, high, preferred_element_type=jnp.float32)
+                     + jnp.dot(pick, middle, preferred_element_type=jnp.float32)
+                     + jnp.dot(pick, low, preferred_element_type=jnp.float32))
+        out_ref[:, pl.ds(pl.multiple_of((side * lane_groups + lane) * LANES, LANES), LANES)] = rows_here
+
+    d_copies = {}
+    for j in order[:-1]:
+        here = full.at[core, z, row]
+        d_copies[j] = send(here, here, d_send.at[j - 1], d_recv.at[j - 1], z_peer(j))
+    e_copies = {}
+    f_copies = {}
+
+    def back_to_core(j):
+        for k in range(1, rows):
+            e_copies[j, k].wait_recv()
+        here = full.at[core, flipped(z, j)]
+        f_copies[j] = send(here, here, f_send.at[j], f_recv.at[j], mate)
+
+    for j in range(zs):
+        if j:
+            d_copies[j].wait_recv()
+        here = full.at[core, flipped(z, j), row]
+        for k in far_rows:
+            e_copies[j, k] = send(here, here, e_send.at[j, k - 1], e_recv.at[j, k - 1], row_peer(k))
+        if j >= 2:
+            back_to_core(j - 2)
+    for j in range(max(zs - 2, 0), zs):
+        back_to_core(j)
+
+    if slabs == 1:
+        for j in range(zs):
+            emit_lane(core, flipped(z, j))
+        for j in range(zs):
+            f_copies[j].wait_recv()
+            emit_lane(other, flipped(z, j))
+    else:
         for lane in range(lane_groups):
-            parts = [full[side, slab, r] for slab in range(lane * slabs, (lane + 1) * slabs) for r in range(rows)]
-            total = jnp.concatenate(parts, axis=0)
-            high = total.astype(jnp.bfloat16)
-            rest = total - high.astype(jnp.float32)
-            middle = rest.astype(jnp.bfloat16)
-            low = (rest - middle.astype(jnp.float32)).astype(jnp.bfloat16)
-            rows_here = (jnp.dot(pick, high, preferred_element_type=jnp.float32)
-                         + jnp.dot(pick, middle, preferred_element_type=jnp.float32)
-                         + jnp.dot(pick, low, preferred_element_type=jnp.float32))
-            lanes = pl.ds(pl.multiple_of((side * lane_groups + lane) * LANES, LANES), LANES)
-            out_ref[:, lanes] = rows_here
-
-    emit(core)
-    for j in range(zs):
-        f_copies[j].wait_recv()
-    emit(other)
+            emit_lane(core, lane)
+        for j in range(zs):
+            f_copies[j].wait_recv()
+        for lane in range(lane_groups):
+            emit_lane(other, lane)
     for copy in sent:
         copy.wait_send()
 
@@ -276,7 +291,7 @@
     dma = pltpu.SemaphoreType.DMA
     return pl.pallas_call(
         functools.partial(sum_kernel, rows, zs, shard),
-        out_shape=jax.ShapeDtypeStruct((shard, width_lanes * LANES), f32),
+        out_shape=pltpu.VMEM((shard, width_lanes * LANES), f32),
         in_specs=[pl.BlockSpec(memory_space=pl.ANY), vmem, pl.BlockSpec(memory_space=pltpu.SMEM)],
         out_specs=vmem,
         scratch_shapes=[

time: 35.2 us -> 32.5 us (0.923)
  Pallas kernels: 32.5 us -> 30.1 us
  other arithmetic: 1.69 us -> 0.74 us
  local copies, waits for them, and re-layouts: 0.01 us -> 0.79 us
    pallas_call x1, Pallas kernels: 25.1 us -> 23.5 us  [sum_part(): pl.pallas_call(functools.partial(sum_kernel, rows, zs, shard), out_shape=...]
    add x1, other arithmetic: 1.69 us -> 0.74 us  [body(): momentum_out = decay_rate * momentum + total_shard / (rows * 2 * zs)]
    unnamed x2 -> x4, local copies, waits for them, and re-layouts: 0.01 us -> 0.79 us
    pallas_call x1, Pallas kernels: 7.39 us -> 6.62 us  [local_part(): pl.pallas_call(functools.partial(local_kernel, chunk), in_specs=[hbm, hbm...]
where the time goes in v4:
time: 32.5 us; the launch traced here: 32.3 us
  Pallas kernels  30.1 us (93%)
  local copies, waits for them, and re-layouts  0.79 us (2%)
  other arithmetic  0.74 us (2%)
  between operations  0.67 us (2%)
    pallas_call x1, Pallas kernels, sum_part(): pl.pallas_call(functools.partial(sum_kernel, rows, zs, shard), out_shape=...  23.5 us
    pallas_call x1, Pallas kernels, local_part(): pl.pallas_call(functools.partial(local_kernel, chunk), in_specs=[hbm, hbm...  6.62 us
    unnamed x4, local copies, waits for them, and re-layouts  0.79 us
    add x1, other arithmetic, body(): momentum_out = decay_rate * momentum + total_shard / (rows * 2 * zs)  0.74 us

profile of v4, /device:TPU:0, one launch (start us, length us, event | category | flops | bytes accessed | tf_op | source)
XLA Modules:
  0.0 32.3 jit_solution(4418722027391296303)
XLA Ops:
  0.6 0.0 copy-start.1
  0.6 6.6 %local.1 = (bf16[2048,1024]{1,0:T(8,128)(2,1)}, f32[8,128,128]{2,1,0:T(8,128)S(1)}) custom-call(bf16[256,4096]{1,0:T(8,128)(2,1)} %tokens_hbm.1, bf16[256,512]{1,0:T(8,128)(2,1)} %grad_hbm.1, bf16[2048,1024]{1,0:T(8,128)(2,1)} %bitcast.6, s32[5,1,128]{2,1,0:T(1,128)} %bitcast.7, s32[5,1,128]{2,1,0:T(1,128)} %bitcast.8, s32[5]{0:T(128)} %bitcast.10), custom_call_target="tpu_custom_call" | custom-call | tf_op jit(solution)/shard_map/local/pallas_call | solution.py:129
  7.3 0.0 copy-start
  7.3 0.8 %copy-done = f32[8,128,128]{2,1,0:T(8,128)} copy-done((f32[8,128,128]{2,1,0:T(8,128)}, f32[8,128,128]{2,1,0:T(8,128)S(1)}, u32[]{:S(2)}) %copy-start) | copy-done | bytes 524312
  8.1 23.5 %total.1 = f32[64,1024]{1,0:T(8,128)S(1)} custom-call(f32[2,4,4,32,128]{4,3,2,1,0:T(8,128)} %bitcast.5, s32[5,1,128]{2,1,0:T(1,128)} %bitcast.9, s32[5]{0:T(128)} %bitcast.11), custom_call_target="tpu_custom_call" | custom-call | tf_op jit(solution)/shard_map/total/pallas_call | solution.py:292
  31.5 0.0 copy-done.1
  31.5 0.7 %multiply_add_fusion = f32[64,1024]{1,0:T(8,128)} fusion(f32[64,1024]{1,0:T(8,128)S(1)} %total.1, f32[64,1024]{1,0:T(8,128)S(1)} %copy-done.1), kind=kLoop, calls=%fused_computation | loop fusion | flops 196608 | bytes 786432 | tf_op jit(solution)/shard_map/add | solution.py:326
Async XLA Ops:
  0.6 30.9 %copy-start.1 = (f32[64,1024]{1,0:T(8,128)S(1)}, f32[64,1024]{1,0:T(8,128)}, u32[]{:S(2)}) copy-start(f32[64,1024]{1,0:T(8,128)} %param.9) | copy-start | bytes 786436
  7.3 0.8 %copy-start = (f32[8,128,128]{2,1,0:T(8,128)}, f32[8,128,128]{2,1,0:T(8,128)S(1)}, u32[]{:S(2)}) copy-start(f32[8,128,128]{2,1,0:T(8,128)S(1)} %get-tuple-element.5) | copy-start | bytes 1572868

commit v5 on v4

--- a/solution.py
+++ b/solution.py
@@ -154,8 +154,8 @@
 
 
 def sum_kernel(rows, zs, shard, packed_ref, lists_ref, counts_ref, out_ref,
-               own, core_in, half, row_in, part, z_in, full,
-               own_sem, a_send, a_recv, b_send, b_recv, c_send, c_recv,
+               core_in, half, row_in, part, z_in, full,
+               a_send, a_recv, b_send, b_recv, c_send, c_recv,
                d_send, d_recv, e_send, e_recv, f_send, f_recv):
     row = lax.axis_index("row")
     col = lax.axis_index("col")
@@ -180,8 +180,6 @@
         sent.append(copy)
         return copy
 
-    own_copy = pltpu.make_async_copy(packed_ref.at[core], own, own_sem)
-    own_copy.start()
     barrier = pltpu.get_barrier_semaphore()
     pl.semaphore_signal(barrier, inc=1, device_id=mate, device_id_type=MESH)
     for k in range(1, rows):
@@ -196,11 +194,10 @@
     for j in order:
         spot = flipped(z, j)
         a_copies[j] = send(packed_ref.at[other, spot], core_in.at[j], a_send.at[j], a_recv.at[j], mate)
-    own_copy.wait()
     b_copies = {}
     for j in order:
         a_copies[j].wait_recv()
-        half[j] = own[flipped(z, j)] + core_in[j]
+        half[j] = packed_ref[core, flipped(z, j)] + core_in[j]
         for k in far_rows:
             b_copies[j, k] = send(half.at[j, flipped(row, k)], row_in.at[j, k - 1],
                                   b_send.at[j, k - 1], b_recv.at[j, k - 1], row_peer(k))
@@ -286,23 +283,22 @@
     width_lanes, capacity, _ = packed.shape
     piece = width_lanes * capacity // (2 * rows * zs)
     packed = packed.reshape(2, zs, rows, piece, LANES)
+    packed = pltpu.with_memory_space_constraint(packed, pltpu.VMEM)
     vmem = pl.BlockSpec(memory_space=pltpu.VMEM)
     f32 = jnp.float32
     dma = pltpu.SemaphoreType.DMA
     return pl.pallas_call(
         functools.partial(sum_kernel, rows, zs, shard),
         out_shape=pltpu.VMEM((shard, width_lanes * LANES), f32),
-        in_specs=[pl.BlockSpec(memory_space=pl.ANY), vmem, pl.BlockSpec(memory_space=pltpu.SMEM)],
+        in_specs=[vmem, vmem, pl.BlockSpec(memory_space=pltpu.SMEM)],
         out_specs=vmem,
         scratch_shapes=[
-            pltpu.VMEM((zs, rows, piece, LANES), f32),
             pltpu.VMEM((zs, rows, piece, LANES), f32),
             pltpu.VMEM((zs, rows, piece, LANES), f32),
             pltpu.VMEM((zs, rows - 1, piece, LANES), f32),
             pltpu.VMEM((zs, piece, LANES), f32),
             pltpu.VMEM((zs - 1, piece, LANES), f32),
             pltpu.VMEM((2, zs, rows, piece, LANES), f32),
-            dma(()),
             dma((zs,)), dma((zs,)),
             dma((zs, rows - 1)), dma((zs, rows - 1)),
             dma((zs - 1,)), dma((zs - 1,)),

time: 32.5 us -> 31.5 us (0.969)
  local copies, waits for them, and re-layouts: 0.79 us -> 0.01 us
    unnamed x4 -> x2, local copies, waits for them, and re-layouts: 0.79 us -> 0.01 us
where the time goes in v5:
time: 31.5 us; the launch traced here: 31.3 us
  Pallas kernels  29.9 us (95%)
  other arithmetic  0.74 us (2%)
  between operations  0.66 us (2%)
    pallas_call x1, Pallas kernels, sum_part(): pl.pallas_call(functools.partial(sum_kernel, rows, zs, shard), out_shape=...  23.3 us
    pallas_call x1, Pallas kernels, local_part(): pl.pallas_call(functools.partial(local_kernel, chunk), in_specs=[hbm, hbm...  6.62 us
    add x1, other arithmetic, body(): momentum_out = decay_rate * momentum + total_shard / (rows * 2 * zs)  0.74 us

profile of v5, /device:TPU:0, one launch (start us, length us, event | category | flops | bytes accessed | tf_op | source)
XLA Modules:
  0.0 31.3 jit_solution(2263690372429506642)
XLA Ops:
  0.6 0.0 copy-start
  0.6 6.6 %local.1 = (bf16[2048,1024]{1,0:T(8,128)(2,1)}, f32[8,128,128]{2,1,0:T(8,128)S(1)}) custom-call(bf16[256,4096]{1,0:T(8,128)(2,1)} %tokens_hbm.1, bf16[256,512]{1,0:T(8,128)(2,1)} %grad_hbm.1, bf16[2048,1024]{1,0:T(8,128)(2,1)} %bitcast.6, s32[5,1,128]{2,1,0:T(1,128)} %bitcast.7, s32[5,1,128]{2,1,0:T(1,128)} %bitcast.8, s32[5]{0:T(128)} %bitcast.10), custom_call_target="tpu_custom_call" | custom-call | tf_op jit(solution)/shard_map/local/pallas_call | solution.py:129
  7.3 23.3 %total.1 = f32[64,1024]{1,0:T(8,128)S(1)} custom-call(f32[2,4,4,32,128]{4,3,2,1,0:T(8,128)S(1)} %bitcast.5, s32[5,1,128]{2,1,0:T(1,128)} %bitcast.9, s32[5]{0:T(128)} %bitcast.11), custom_call_target="tpu_custom_call" | custom-call | tf_op jit(solution)/shard_map/total/pallas_call | solution.py:290
  30.5 0.0 copy-done
  30.6 0.7 %multiply_add_fusion = f32[64,1024]{1,0:T(8,128)} fusion(f32[64,1024]{1,0:T(8,128)S(1)} %total.1, f32[64,1024]{1,0:T(8,128)S(1)} %copy-done), kind=kLoop, calls=%fused_computation | loop fusion | flops 196608 | bytes 786432 | tf_op jit(solution)/shard_map/add | solution.py:322
Async XLA Ops:
  0.6 29.9 %copy-start = (f32[64,1024]{1,0:T(8,128)S(1)}, f32[64,1024]{1,0:T(8,128)}, u32[]{:S(2)}) copy-start(f32[64,1024]{1,0:T(8,128)} %param.9) | copy-start | bytes 786436

commit v6 on v5

--- a/solution.py
+++ b/solution.py
@@ -99,10 +99,11 @@
                 total = grads[side * (sub // 2):(side + 1) * (sub // 2)] + values[rows, columns].astype(jnp.float32)
                 acc[rows, columns] = total
                 values[rows, columns] = jnp.where(kept_row, 0.0, total).astype(jnp.bfloat16)
-        rows, _ = spans(step)
-        copy = pltpu.make_async_copy(values.at[rows], out_hbm.at[rows], out_sems.at[step])
-        copy.start()
-        out_copies.append(copy)
+            if piece % 2 == 1:
+                done = slice(start - sub // 2, start + sub // 2)
+                copy = pltpu.make_async_copy(values.at[done], out_hbm.at[done], out_sems.at[len(out_copies)])
+                copy.start()
+                out_copies.append(copy)
 
     list_copy.wait()
 
@@ -143,7 +144,7 @@
             pltpu.VMEM((blocks, width), jnp.float32),
             pltpu.VMEM((capacity, width), jnp.float32),
             pltpu.SMEM((sections, 1, capacity), jnp.int32),
-            dma((steps,)), dma((steps,)), dma((steps,)), dma(()), dma(()),
+            dma((steps,)), dma((steps,)), dma((blocks // 256,)), dma(()), dma(()),
         ],
         out_shape=[
             jax.ShapeDtypeStruct((blocks, width), jnp.bfloat16),
@@ -246,10 +247,11 @@
     f_copies = {}
 
     def back_to_core(j):
-        for k in range(1, rows):
-            e_copies[j, k].wait_recv()
-        here = full.at[core, flipped(z, j)]
-        f_copies[j] = send(here, here, f_send.at[j], f_recv.at[j], mate)
+        for k in range(rows):
+            if k:
+                e_copies[j, k].wait_recv()
+            here = full.at[core, flipped(z, j), flipped(row, k)]
+            f_copies[j, k] = send(here, here, f_send.at[j, k], f_recv.at[j, k], mate)
 
     for j in range(zs):
         if j:
@@ -266,13 +268,15 @@
         for j in range(zs):
             emit_lane(core, flipped(z, j))
         for j in range(zs):
-            f_copies[j].wait_recv()
+            for k in range(rows):
+                f_copies[j, k].wait_recv()
             emit_lane(other, flipped(z, j))
     else:
         for lane in range(lane_groups):
             emit_lane(core, lane)
         for j in range(zs):
-            f_copies[j].wait_recv()
+            for k in range(rows):
+                f_copies[j, k].wait_recv()
         for lane in range(lane_groups):
             emit_lane(other, lane)
     for copy in sent:
@@ -304,7 +308,7 @@
             dma((zs - 1,)), dma((zs - 1,)),
             dma((zs - 1,)), dma((zs - 1,)),
             dma((zs, rows - 1)), dma((zs, rows - 1)),
-            dma((zs,)), dma((zs,)),
+            dma((zs, rows)), dma((zs, rows)),
         ],
         compiler_params=pltpu.CompilerParams(collective_id=0, has_side_effects=True),
         name="total",

time: 31.5 us -> 31.6 us (level)
  no operation moved by 1% of the time
where the time goes in v6:
time: 31.6 us; the launch traced here: 31.4 us
  Pallas kernels  30 us (95%)
  other arithmetic  0.74 us (2%)
  between operations  0.66 us (2%)
    pallas_call x1, Pallas kernels, sum_part(): pl.pallas_call(functools.partial(sum_kernel, rows, zs, shard), out_shape=...  23.5 us
    pallas_call x1, Pallas kernels, local_part(): pl.pallas_call(functools.partial(local_kernel, chunk), in_specs=[hbm, hbm...  6.5 us
    add x1, other arithmetic, body(): momentum_out = decay_rate * momentum + total_shard / (rows * 2 * zs)  0.74 us

profile of v6, /device:TPU:0, one launch (start us, length us, event | category | flops | bytes accessed | tf_op | source)
XLA Modules:
  0.0 31.4 jit_solution(11968146262808164618)
XLA Ops:
  0.6 0.0 copy-start
  0.6 6.5 %local.1 = (bf16[2048,1024]{1,0:T(8,128)(2,1)}, f32[8,128,128]{2,1,0:T(8,128)S(1)}) custom-call(bf16[256,4096]{1,0:T(8,128)(2,1)} %tokens_hbm.1, bf16[256,512]{1,0:T(8,128)(2,1)} %grad_hbm.1, bf16[2048,1024]{1,0:T(8,128)(2,1)} %bitcast.6, s32[5,1,128]{2,1,0:T(1,128)} %bitcast.7, s32[5,1,128]{2,1,0:T(1,128)} %bitcast.8, s32[5]{0:T(128)} %bitcast.10), custom_call_target="tpu_custom_call" | custom-call | tf_op jit(solution)/shard_map/local/pallas_call | solution.py:130
  7.1 23.5 %total.1 = f32[64,1024]{1,0:T(8,128)S(1)} custom-call(f32[2,4,4,32,128]{4,3,2,1,0:T(8,128)S(1)} %bitcast.5, s32[5,1,128]{2,1,0:T(1,128)} %bitcast.9, s32[5]{0:T(128)} %bitcast.11), custom_call_target="tpu_custom_call" | custom-call | tf_op jit(solution)/shard_map/total/pallas_call | solution.py:294
  30.7 0.0 copy-done
  30.7 0.7 %multiply_add_fusion = f32[64,1024]{1,0:T(8,128)} fusion(f32[64,1024]{1,0:T(8,128)S(1)} %total.1, f32[64,1024]{1,0:T(8,128)S(1)} %copy-done), kind=kLoop, calls=%fused_computation | loop fusion | flops 196608 | bytes 786432 | tf_op jit(solution)/shard_map/add | solution.py:326
Async XLA Ops:
  0.6 30.0 %copy-start = (f32[64,1024]{1,0:T(8,128)S(1)}, f32[64,1024]{1,0:T(8,128)}, u32[]{:S(2)}) copy-start(f32[64,1024]{1,0:T(8,128)} %param.9) | copy-start | bytes 786436
